TPU v7x, 128 devices: a whole 4x4x4 slice. The times are simulated.
128 devices in a mesh: segment: 8 (over y, x_hi), tp: 16 (over x_lo, z, core).
Axes of the slice: x: 4 (x_hi: 2, x_lo: 2; x = x_hi * 2 + x_lo), y: 4, z: 4, core: 2. Of those that a mesh axis runs over, the one named last changes fastest.
Arguments:
- memory: bfloat16 [1024, 4096], P('segment', 'tp'), may hold values from -6 to 6
- norm_gain: float32 [4096], replicated, may hold values from 0.1 to 1.9
- queries: bfloat16 [8, 1024, 4096], P('segment', None, 'tp'), may hold values from -200 to 200
- key_weight: bfloat16 [8, 4096, 4096], P('segment', None, 'tp'), may hold values from -0.09375 to 0.09375
- value_weight: bfloat16 [8, 4096, 4096], P('segment', None, 'tp'), may hold values from -0.09375 to 0.09375
- context_grad: bfloat16 [8, 1024, 4096], P('segment', None, 'tp'), may hold values from -6 to 6
Outputs:
- context: bfloat16 [8, 1024, 4096], P('segment', None, 'tp')
- query_grad: bfloat16 [8, 1024, 4096], P('segment', None, 'tp')
- key_weight_grad: float32 [8, 4096, 4096], P('segment', None, 'tp')
- value_weight_grad: float32 [8, 4096, 4096], P('segment', None, 'tp')
- encoder_output_gradient: float32 [1024, 4096], P('segment', 'tp')
All inputs are finite; a program needn't handle non-finite values.
Results may differ from a plain program's by a relative error of at most 0.015.
The roundings to bfloat16 on the way count: a program that leaves them out, or rounds other values in their place, can miss the bound.
Values may be sent and summed in bfloat16 or wider, within the bound.
No kernel may reach another device: no remote copies, remote signals or barrier semaphores. Data moves between devices by JAX's collectives and lax.ppermute only.
A program may use at most 128 MiB of HBM per device.

v0:
```python
import jax
import jax.numpy as jnp
from jax import lax
from jax.sharding import PartitionSpec as P

HD = 256


def joined_along(pieces, dim):
    pieces = jnp.moveaxis(pieces, 0, dim)
    shape = pieces.shape
    return pieces.reshape(*shape[:dim], shape[dim] * shape[dim + 1], *shape[dim + 2 :])


def sent_to_all(value, axis):
    copies = jnp.broadcast_to(value, (lax.axis_size(axis), *value.shape))
    return lax.all_to_all(copies, axis, split_axis=0, concat_axis=0, tiled=True)


def collect(value, axis, dim):
    return joined_along(sent_to_all(value, axis), dim)


def of_everyone(value, axis):
    return sent_to_all(value, axis).sum(axis=0)


def in_blocks(value, dim, size):
    before, after = (value.shape[:dim], value.shape[dim + 1 :])
    return jnp.moveaxis(value.reshape(*before, size, -1, *after), dim, 0)


def summed_on_arrival(value, axis, dim):
    size = lax.axis_size(axis)
    pieces = lax.all_to_all(in_blocks(value, dim, size), axis, 0, 0, tiled=True)
    return jnp.sum(pieces.astype(jnp.float32), axis=0)


def local(memory, norm_gain, queries, key_weight, value_weight, context_grad):
    epsilon_value = 1e-06
    hidden_width = norm_gain.shape[0]
    piece_cols = memory.shape[1]
    rows_own = memory.shape[0]
    tp_index = lax.axis_index("tp")
    segment_index = lax.axis_index("segment")
    own_gain = lax.dynamic_slice_in_dim(norm_gain, tp_index * piece_cols, piece_cols)
    local_row_block = memory.astype(jnp.float32)
    gathered = collect(memory, "segment", 0)
    source_all = gathered.astype(jnp.float32)
    squares = of_everyone(jnp.sum(source_all * source_all, axis=1), "tp")
    scale_all = lax.rsqrt(squares / hidden_width + epsilon_value)
    normed_piece = (source_all * scale_all[:, None] * own_gain).astype(jnp.bfloat16)
    normed = lax.all_gather(normed_piece, "tp", axis=1, tiled=True)
    local_scale = lax.dynamic_slice_in_dim(scale_all, segment_index * rows_own, rows_own)
    key_mat = key_weight[0]
    value_mat = value_weight[0]
    query_rows = queries[0]
    dctx = context_grad[0]
    source_count = normed.shape[0]
    target_count = query_rows.shape[0]
    head_count = key_mat.shape[1] // HD
    scale = HD ** (-0.5)
    key_rows = jnp.dot(normed, key_mat, preferred_element_type=jnp.float32).astype(jnp.bfloat16)
    value_rows = jnp.dot(normed, value_mat, preferred_element_type=jnp.float32).astype(jnp.bfloat16)
    qh = query_rows.reshape(target_count, head_count, HD)
    kh = key_rows.reshape(source_count, head_count, HD)
    vh = value_rows.reshape(source_count, head_count, HD)
    dch = dctx.reshape(target_count, head_count, HD)
    scores = jnp.einsum("qhd,khd->hqk", qh, kh, preferred_element_type=jnp.float32) * scale
    maxima = jnp.max(scores, axis=-1, keepdims=True)
    exponent = jnp.exp(scores - maxima)
    attend = exponent / jnp.sum(exponent, axis=-1, keepdims=True)
    attend_low = attend.astype(jnp.bfloat16)
    context = jnp.einsum("hqk,khd->qhd", attend_low, vh, preferred_element_type=jnp.float32).astype(
        jnp.bfloat16
    )
    grad_attend = jnp.einsum("qhd,khd->hqk", dch, vh, preferred_element_type=jnp.float32)
    row_dots = jnp.sum(grad_attend * attend, axis=-1, keepdims=True)
    grad_scores = (attend * (grad_attend - row_dots) * scale).astype(jnp.bfloat16)
    query_grad = jnp.einsum(
        "hqk,khd->qhd", grad_scores, kh, preferred_element_type=jnp.float32
    ).astype(jnp.bfloat16)
    grad_keys = jnp.einsum(
        "hqk,qhd->khd", grad_scores, qh, preferred_element_type=jnp.float32
    ).astype(jnp.bfloat16)
    grad_values = jnp.einsum(
        "hqk,qhd->khd", attend_low, dch, preferred_element_type=jnp.float32
    ).astype(jnp.bfloat16)
    grad_keys = grad_keys.reshape(source_count, head_count * HD)
    grad_values = grad_values.reshape(source_count, head_count * HD)
    key_grad = jnp.einsum("sd,sc->dc", normed, grad_keys, preferred_element_type=jnp.float32)
    value_grad = jnp.einsum("sd,sc->dc", normed, grad_values, preferred_element_type=jnp.float32)
    total = jnp.einsum("sc,dc->sd", grad_keys, key_mat, preferred_element_type=jnp.float32)
    segment_part = lax.psum_scatter(
        (
            total
            + jnp.einsum("sc,dc->sd", grad_values, value_mat, preferred_element_type=jnp.float32)
        ).astype(jnp.bfloat16),
        "segment",
        scatter_dimension=0,
        tiled=True,
    )
    summed = summed_on_arrival(segment_part, "tp", 1)
    upper_term = summed * own_gain
    centered_normalized = local_row_block * local_scale[:, None]
    inner_product = of_everyone(jnp.sum(upper_term * centered_normalized, axis=1), "tp")
    encoder_output_gradient = local_scale[:, None] * (
        upper_term - centered_normalized * (inner_product / hidden_width)[:, None]
    )
    return (
        context.reshape(1, target_count, head_count * HD),
        query_grad.reshape(1, target_count, head_count * HD),
        key_grad[None],
        value_grad[None],
        encoder_output_gradient,
    )


def solution(mesh):
    placed = (
        P("segment", "tp"),
        P(),
        P("segment", None, "tp"),
        P("segment", None, "tp"),
        P("segment", None, "tp"),
        P("segment", None, "tp"),
    )
    return jax.shard_map(
        local,
        mesh=mesh,
        in_specs=placed,
        out_specs=(
            P("segment", None, "tp"),
            P("segment", None, "tp"),
            P("segment", None, "tp"),
            P("segment", None, "tp"),
            P("segment", "tp"),
        ),
        check_vma=False,
    )
```

profile of v0, /device:TPU:1, one launch (start us, length us, event | category | flops | bytes accessed | tf_op | source)
XLA Modules:
  0.0 292.4 jit_solution(10155391424537069540)
XLA Ops:
  7.2 0.0 copy-start
  7.2 1.0 broadcast_in_dim.12
  8.2 18.0 %all_to_all.22 = bf16[8,128,256]{2,1,0:T(8,128)(2,1)S(1)} all-to-all(bf16[8,128,256]{2,1,0:T(8,128)(2,1)S(1)} %broadcast_in_dim.12), channel_id=1, replica_groups=mesh['segment'=8,'tp'=16] {'segment'}, dimensions={0} | all-to-all | bytes 1048576 | tf_op jit(solution)/shard_map/all_to_all | solution.py:17
  26.2 0.2 multiply_reduce_fusion.1
  26.4 0.7 broadcast_in_dim.28
  27.0 7.2 %all-to-all-start.1 = ((f32[16,1,1024]{2,1,0:T(1,128)}), f32[16,1,1024]{2,1,0:T(1,128)S(1)}, u32[]{:S(2)}, u32[]{:S(2)}) async-start(f32[16,1,1024]{2,1,0:T(1,128)} %broadcast_in_dim.28), calls=%async_computation.1 | async-start | bytes 131072 | tf_op jit(solution)/shard_map/all_to_all | solution.py:17
  34.3 0.0 all-gather.2.cloned.1.call-start
  34.3 0.8 dynamic_slice.6
  35.1 5.0 %all-to-all-done.1 = f32[16,1,1024]{2,1,0:T(1,128)S(1)} async-done(((f32[16,1,1024]{2,1,0:T(1,128)}), f32[16,1,1024]{2,1,0:T(1,128)S(1)}, u32[]{:S(2)}, u32[]{:S(2)}) %all-to-all-start.1) | async-done | bytes 65568 | tf_op jit(solution)/shard_map/all_to_all | solution.py:17
  40.1 0.1 reduce_sum.64
  40.2 1.0 fusion.22
  41.2 0.0 all-gather.2.cloned.1.call-update
  41.2 0.0 copy-start.7
  41.2 0.0 reduce-scatter.2.cloned.1.call-start
  41.2 57.2 %all-gather.2.cloned.1.call-done = bf16[1024,4096]{1,0:T(8,128)(2,1)} async-done(((bf16[1024,256]{1,0:T(8,128)(2,1)}), bf16[1024,4096]{1,0:T(8,128)(2,1)}) %all-gather.2.cloned.1.call-update) | async-done | bytes 8388624 | tf_op jit(solution)/shard_map/all_gather | solution.py:53
  98.4 0.0 copy-done
  98.4 5.7 %fusion.16 = bf16[1024,256]{1,0:T(8,128)(2,1)S(1)} fusion(bf16[1024,4096]{1,0:T(8,128)(2,1)} %all-gather.2.cloned.1.call-done, bf16[1,4096,256]{2,1,0:T(8,128)(2,1)S(1)} %copy-done), kind=kOutput, calls=%fused_computation.23 | convolution fusion | flops 2147745792 | bytes 11010048 | tf_op jit(solution)/shard_map/dot_general | solution.py:63
  104.1 0.0 copy-done.7
  104.1 0.0 copy-start.4
  104.1 0.0 copy-start.10
  104.2 0.8 multiply_reduce_fusion
  104.9 0.0 copy-start.2
  104.9 0.0 slice-start
  104.9 0.7 fusion.5
  105.7 0.0 copy-done.4
  105.7 0.0 copy-done.10
  105.7 0.0 copy-start.5
  105.7 0.0 slice-start.1
  105.7 1.0 convolution_convert_fusion
  106.7 2.0 slice-done
  108.7 0.6 copy-done.5
  109.3 1.2 slice-done.1
  110.5 2.3 fusion.13
  112.8 0.0 copy-start.11
  112.9 1.5 fusion
  114.4 0.0 copy-done.11
  114.4 0.0 copy-done.2
  114.4 1.3 fusion.3
  115.7 0.0 copy-start.3
  115.7 1.3 copy-done.3
  117.0 0.7 convolution_convert_fusion.1
  117.7 8.1 %fusion.6 = f32[1024,4096]{1,0:T(8,128)} fusion(bf16[1024,256]{1,0:T(8,128)(2,1)S(1)} %convolution_convert_fusion.1, bf16[1,4096,256]{2,1,0:T(8,128)(2,1)S(1)} %copy-done), kind=kOutput, calls=%fused_computation.14 | convolution fusion | flops 2147483648 | bytes 19398656 | tf_op jit(solution)/shard_map/sc,dc->sd/dot_general | solution.py:93
  125.8 0.0 copy-done.8
  125.8 11.6 %add_convert_fusion = bf16[1024,4096]{1,0:T(8,128)(2,1)} fusion(f32[1024,4096]{1,0:T(8,128)} %fusion.6, bf16[1024,256]{1,0:T(8,128)(2,1)S(1)} %convolution_convert_fusion, bf16[1,4096,256]{2,1,0:T(8,128)(2,1)S(1)} %copy-done.5), kind=kOutput, calls=%fused_computation | convolution fusion | flops 2155872256 | bytes 27787264 | tf_op jit(solution)/shard_map/sc,dc->sd/dot_general | solution.py:97
  137.4 0.0 reduce-scatter.2.cloned.1.call-update
  137.4 0.1 dynamic_slice.7
  137.5 7.8 %convolution_bitcast_fusion.1 = f32[1,4096,256]{2,1,0:T(8,128)} fusion(bf16[1024,4096]{1,0:T(8,128)(2,1)} %all-gather.2.cloned.1.call-done, bf16[1024,256]{1,0:T(8,128)(2,1)S(1)} %convolution_convert_fusion.1), kind=kOutput, calls=%fused_computation.2 | convolution fusion | flops 2147483648 | bytes 13107200 | tf_op jit(solution)/shard_map/sd,sc->dc/dot_general | solution.py:91
  145.3 104.9 %reduce-scatter.2.cloned.1.call-done = bf16[128,4096]{1,0:T(8,128)(2,1)} async-done(((bf16[1024,4096]{1,0:T(8,128)(2,1)}), bf16[128,4096]{1,0:T(8,128)(2,1)}) %reduce-scatter.2.cloned.1.call-update) | async-done | bytes 1048592 | tf_op jit(solution)/shard_map/reduce_scatter | solution.py:94
  250.2 2.4 copy.31
  252.6 5.7 %all-to-all-start.2 = ((bf16[16,128,256]{2,1,0:T(8,128)(2,1)}), bf16[16,128,256]{2,1,0:T(8,128)(2,1)S(1)}, u32[]{:S(2)}, u32[]{:S(2)}) async-start(bf16[16,128,256]{2,1,0:T(8,128)(2,1)} %bitcast.89), calls=%async_computation.3 | async-start | bytes 2097152 | tf_op jit(solution)/shard_map/all_to_all | solution.py:35
  258.3 0.0 copy-done.12
  258.3 4.2 %fusion.19 = bf16[1,1024,256]{1,2,0:T(8,128)(2,1)} fusion(bf16[1024,256]{1,0:T(8,128)(2,1)S(1)} %copy-done.12, f32[1024,1024]{1,0:T(8,128)} %copy-done.2, f32[1024]{0:T(1024)S(1)} %fusion.5, f32[1024]{0:T(1024)S(1)} %get-tuple-element.25), kind=kOutput, calls=%fused_computation.28 | convolution fusion | flops 541327360 | bytes 5251072 | tf_op jit(solution)/shard_map/hqk,khd->qhd/dot_general | solution.py:74
  262.5 8.0 %convolution_bitcast_fusion = f32[1,4096,256]{2,1,0:T(8,128)} fusion(bf16[1024,4096]{1,0:T(8,128)(2,1)} %all-gather.2.cloned.1.call-done, bf16[1024,256]{1,0:T(8,128)(2,1)S(1)} %copy-done.9), kind=kOutput, calls=%fused_computation.1 | convolution fusion | flops 2147483648 | bytes 13107200 | tf_op jit(solution)/shard_map/sd,sc->dc/dot_general | solution.py:92
  270.5 3.6 %all-to-all-done.2 = bf16[16,128,256]{2,1,0:T(8,128)(2,1)S(1)} async-done(((bf16[16,128,256]{2,1,0:T(8,128)(2,1)}), bf16[16,128,256]{2,1,0:T(8,128)(2,1)S(1)}, u32[]{:S(2)}, u32[]{:S(2)}) %all-to-all-start.2) | async-done | bytes 1048608 | tf_op jit(solution)/shard_map/all_to_all | solution.py:35
  274.1 0.1 convert_reduce_fusion
  274.3 0.0 copy-done.6
  274.3 0.2 multiply_reduce_fusion.2
  274.5 0.6 broadcast_in_dim.31
  275.1 4.1 %all-to-all-start.3 = ((f32[16,1,128]{2,1,0:T(1,128)}), f32[16,1,128]{2,1,0:T(1,128)S(1)}, u32[]{:S(2)}, u32[]{:S(2)}) async-start(f32[16,1,128]{2,1,0:T(1,128)} %broadcast_in_dim.31), calls=%async_computation.4 | async-start | bytes 16384 | tf_op jit(solution)/shard_map/all_to_all | solution.py:17
  279.2 2.5 fusion.20
  281.7 2.0 copy.26
  283.7 1.0 copy.27
  284.7 0.0 all-to-all-done.3
  284.8 0.8 subtract_multiply_fusion
  (11 shorter events, 0.0 us)
Async XLA Ops:
  7.2 91.2 %copy-start = (bf16[1,4096,256]{2,1,0:T(8,128)(2,1)S(1)}, bf16[1,4096,256]{2,1,0:T(8,128)(2,1)}, u32[]{:S(2)}) copy-start(bf16[1,4096,256]{2,1,0:T(8,128)(2,1)} %param.9) | copy-start | bytes 6291460
  27.0 13.0 %all-to-all-start.1 = ((f32[16,1,1024]{2,1,0:T(1,128)}), f32[16,1,1024]{2,1,0:T(1,128)S(1)}, u32[]{:S(2)}, u32[]{:S(2)}) async-start(f32[16,1,1024]{2,1,0:T(1,128)} %broadcast_in_dim.28), calls=%async_computation.1 | async-start | bytes 131072 | tf_op jit(solution)/shard_map/all_to_all | solution.py:17
  34.3 64.1 %all-gather.2.cloned.1.call-start = ((), (), s32[]{:S(2)}) async-start(), calls=%async_computation.5 | async-start | bytes 8912896 | tf_op jit(solution)/shard_map/all_gather | solution.py:53
  41.2 62.9 %copy-start.7 = (bf16[1,1024,256]{2,1,0:T(8,128)(2,1)S(1)}, bf16[1,1024,256]{2,1,0:T(8,128)(2,1)}, u32[]{:S(2)}) copy-start(bf16[1,1024,256]{2,1,0:T(8,128)(2,1)} %param.8) | copy-start | bytes 1572868
  41.2 209.0 %reduce-scatter.2.cloned.1.call-start = ((), (), s32[]{:S(2)}) async-start(), calls=%async_computation.6 | async-start | bytes 9437184 | tf_op jit(solution)/shard_map/reduce_scatter | solution.py:94
  104.1 1.5 copy-start.4
  104.1 1.5 copy-start.10
  104.9 9.5 %copy-start.2 = (f32[1024,1024]{1,0:T(8,128)}, f32[1024,1024]{1,0:T(8,128)S(1)}, u32[]{:S(2)}) copy-start(f32[1024,1024]{1,0:T(8,128)S(1)} %get-tuple-element.26) | copy-start | bytes 12582916
  104.9 3.7 %slice-start = ((s8[8388608]{0:T(1024)(128)(4,1)}), s8[4194304]{0:T(1024)(128)(4,1)S(1)}, s32[]{:S(2)}) async-start(s8[8388608]{0:T(1024)(128)(4,1)} %bitcast.93), calls=%async_computation.7 | async-start | bytes 8388608
  105.7 3.6 %copy-start.5 = (bf16[1,4096,256]{2,1,0:T(8,128)(2,1)S(1)}, bf16[1,4096,256]{2,1,0:T(8,128)(2,1)}, u32[]{:S(2)}) copy-start(bf16[1,4096,256]{2,1,0:T(8,128)(2,1)} %param.10) | copy-start | bytes 6291460
  105.7 4.8 %slice-start.1 = ((s8[8388608]{0:T(1024)(128)(4,1)}), s8[4194304]{0:T(1024)(128)(4,1)S(1)}, s32[]{:S(2)}) async-start(s8[8388608]{0:T(1024)(128)(4,1)} %bitcast.93), calls=%async_computation.8 | async-start | bytes 8388608
  110.5 15.3 %copy-start.8 = (bf16[1024,256]{1,0:T(8,128)(2,1)}, bf16[1024,256]{1,0:T(8,128)(2,1)S(1)}, u32[]{:S(2)}) copy-start(bf16[1024,256]{1,0:T(8,128)(2,1)S(1)} %convolution_convert_fusion) | copy-start | bytes 1572868
  112.8 1.5 copy-start.11
  115.7 1.3 copy-start.3
  145.3 113.0 %copy-start.12 = (bf16[1024,256]{1,0:T(8,128)(2,1)S(1)}, bf16[1024,256]{1,0:T(8,128)(2,1)}, u32[]{:S(2)}) copy-start(bf16[1024,256]{1,0:T(8,128)(2,1)} %copy-done.11) | copy-start | bytes 1572868
  252.6 21.5 %all-to-all-start.2 = ((bf16[16,128,256]{2,1,0:T(8,128)(2,1)}), bf16[16,128,256]{2,1,0:T(8,128)(2,1)S(1)}, u32[]{:S(2)}, u32[]{:S(2)}) async-start(bf16[16,128,256]{2,1,0:T(8,128)(2,1)} %bitcast.89), calls=%async_computation.3 | async-start | bytes 2097152 | tf_op jit(solution)/shard_map/all_to_all | solution.py:35
  258.3 4.2 %copy-start.9 = (bf16[1024,256]{1,0:T(8,128)(2,1)S(1)}, bf16[1024,256]{1,0:T(8,128)(2,1)}, u32[]{:S(2)}) copy-start(bf16[1024,256]{1,0:T(8,128)(2,1)} %copy-done.8) | copy-start | bytes 1572868
  262.5 11.8 %copy-start.6 = (bf16[128,256]{1,0:T(8,128)(2,1)S(1)}, bf16[128,256]{1,0:T(8,128)(2,1)}, u32[]{:S(2)}) copy-start(bf16[128,256]{1,0:T(8,128)(2,1)} %param.6) | copy-start | bytes 196612
  262.5 23.1 %copy-start.1 = (bf16[1,4096,256]{2,1,0:T(8,128)(2,1)S(1)}, bf16[1,4096,256]{2,1,0:T(8,128)(2,1)}, u32[]{:S(2)}) copy-start(bf16[1,4096,256]{2,1,0:T(8,128)(2,1)} %param.9) | copy-start | bytes 6291460
  275.1 9.7 %all-to-all-start.3 = ((f32[16,1,128]{2,1,0:T(1,128)}), f32[16,1,128]{2,1,0:T(1,128)S(1)}, u32[]{:S(2)}, u32[]{:S(2)}) async-start(f32[16,1,128]{2,1,0:T(1,128)} %broadcast_in_dim.31), calls=%async_computation.4 | async-start | bytes 16384 | tf_op jit(solution)/shard_map/all_to_all | solution.py:17
Sparse Core Ops, SparseCore 0:
  41.3 57.0 all-gather.1
  137.5 112.6 reduce-scatter.1
where the time goes:
time: 293 us; the launch traced here: 292 us
  waiting for transfers between devices  171 us (58%)
  matrix products  54.2 us (18%)
  blocking collectives  18 us (6%)
  starting transfers between devices  17.1 us (6%)
  between operations  14.3 us (5%)
  local copies, waits for them, and re-layouts  13.8 us (5%)
  other arithmetic  4.37 us (1%)
    reduce_scatter x1, waiting for transfers between devices, local(): lax.psum_scatter((total + jnp.einsum('sc,dc->sd', grad_values, value_mat,...  105 us
    all_gather x1, waiting for transfers between devices, local(): normed = lax.all_gather(normed_piece, 'tp', axis=1, tiled=True)  57.2 us
    all_to_all x1, blocking collectives, sent_to_all(): return lax.all_to_all(copies, axis, split_axis=0, concat_axis=0, tiled=True)  18 us
    dot_general x1, matrix products, local(): jnp.einsum('sc,dc->sd', grad_values, value_mat, preferred_element_type=jn...  11.6 us
    all_to_all x2, starting transfers between devices, sent_to_all(): return lax.all_to_all(copies, axis, split_axis=0, concat_axis=0, tiled=True)  11.3 us
    unnamed x32, local copies, waits for them, and re-layouts  8.26 us
    dot_general x1, matrix products, local(): jnp.einsum('sc,dc->sd', grad_keys, key_mat, preferred_element_type=jnp.fl...  8.1 us
    dot_general x1, matrix products, local(): jnp.einsum('sd,sc->dc', normed, grad_values, preferred_element_type=jnp.f...  8.01 us
  transfers between devices with their start and end apart: 5, of which 4 were waited for; matrix products, arithmetic and copies ran while one was open for 9% of the time, Pallas kernels for 0%

commit v1 on v0

--- a/solution.py
+++ b/solution.py
@@ -50,7 +50,11 @@
     squares = of_everyone(jnp.sum(source_all * source_all, axis=1), "tp")
     scale_all = lax.rsqrt(squares / hidden_width + epsilon_value)
     normed_piece = (source_all * scale_all[:, None] * own_gain).astype(jnp.bfloat16)
-    normed = lax.all_gather(normed_piece, "tp", axis=1, tiled=True)
+    pages = []
+    for _ in range(jax.lax.psum(1, "tp")):
+        pages.append(normed_piece)
+    base_arr = jax.lax.all_to_all(jnp.stack(pages), "tp", 0, 0)
+    normed = jnp.concatenate(base_arr, axis=1)
     local_scale = lax.dynamic_slice_in_dim(scale_all, segment_index * rows_own, rows_own)
     key_mat = key_weight[0]
     value_mat = value_weight[0]

time: 293 us -> 326 us (1.11)
  blocking collectives: 18 us -> 115 us
  waiting for transfers between devices: 171 us -> 113 us
  matrix products: 54.2 us -> 48.1 us
    all_to_all x0 -> x1, blocking collectives: none -> 97.1 us  [local(): base_arr = jax.lax.all_to_all(jnp.stack(pages), 'tp', 0, 0)]
    all_gather x1 -> x0, waiting for transfers between devices: 57.2 us -> none  [local(): normed = lax.all_gather(normed_piece, 'tp', axis=1, tiled=True)]
    reduce_scatter x1, waiting for transfers between devices: 105 us -> 102 us  [local(): lax.psum_scatter((total + jnp.einsum('sc,dc->sd', grad_values, value_mat,...]
    dot_general x1, matrix products: 5.7 us -> 2.42 us  [local(): jnp.dot(normed, key_mat, preferred_element_type=jnp.float32)]
    unnamed x32 -> x31, local copies, waits for them, and re-layouts: 8.26 us -> 7.53 us
  transfers between devices with their start and end apart: 5 -> 4, of which waited for: 4 -> 4; matrix products, arithmetic and copies ran while one was open for 9% -> 7% of each run, Pallas kernels for 0% -> 0%
where the time goes in v1:
time: 326 us
  blocking collectives  115 us (35%)
  waiting for transfers between devices  113 us (35%)
  matrix products  48.1 us (15%)
  starting transfers between devices  17.1 us (5%)
  between operations  14.3 us (4%)
  local copies, waits for them, and re-layouts  13.6 us (4%)
  other arithmetic  4.81 us (1%)
    reduce_scatter x1, waiting for transfers between devices, local(): lax.psum_scatter((total + jnp.einsum('sc,dc->sd', grad_values, value_mat,...  102 us
    all_to_all x1, blocking collectives, local(): base_arr = jax.lax.all_to_all(jnp.stack(pages), 'tp', 0, 0)  97.1 us
    all_to_all x1, blocking collectives, sent_to_all(): return lax.all_to_all(copies, axis, split_axis=0, concat_axis=0, tiled=True)  18 us
    dot_general x1, matrix products, local(): jnp.einsum('sc,dc->sd', grad_values, value_mat, preferred_element_type=jn...  11.4 us
    all_to_all x2, starting transfers between devices, sent_to_all(): return lax.all_to_all(copies, axis, split_axis=0, concat_axis=0, tiled=True)  11.3 us
    dot_general x1, matrix products, local(): jnp.einsum('sc,dc->sd', grad_keys, key_mat, preferred_element_type=jnp.fl...  8.1 us
    dot_general x1, matrix products, local(): jnp.einsum('sd,sc->dc', normed, grad_values, preferred_element_type=jnp.f...  7.89 us
    dot_general x1, matrix products, local(): jnp.einsum('sd,sc->dc', normed, grad_keys, preferred_element_type=jnp.flo...  7.74 us
  transfers between devices with their start and end apart: 4, of which 4 were waited for; matrix products, arithmetic and copies ran while one was open for 7% of the time, Pallas kernels for 0%

profile of v1, /device:TPU:1, one launch (start us, length us, event | category | flops | bytes accessed | tf_op | source)
XLA Modules:
  0.0 325.7 jit_solution(2254289203654126806)
XLA Ops:
  7.2 0.0 copy-start
  7.2 1.1 copy.37
  8.3 0.1 broadcast_in_dim.12
  8.4 18.0 %all_to_all.27 = bf16[8,128,256]{1,2,0:T(8,128)(2,1)S(1)} all-to-all(bf16[8,128,256]{1,2,0:T(8,128)(2,1)S(1)} %broadcast_in_dim.12), channel_id=1, replica_groups=mesh['segment'=8,'tp'=16] {'segment'}, dimensions={0} | all-to-all | bytes 1048576 | tf_op jit(solution)/shard_map/all_to_all | solution.py:17
  26.3 0.2 copy.38
  26.5 0.2 multiply_reduce_fusion.1
  26.8 0.7 broadcast_in_dim.28
  27.4 7.2 %all-to-all-start.1 = ((f32[16,1,1024]{2,1,0:T(1,128)}), f32[16,1,1024]{2,1,0:T(1,128)S(1)}, u32[]{:S(2)}, u32[]{:S(2)}) async-start(f32[16,1,1024]{2,1,0:T(1,128)} %broadcast_in_dim.28), calls=%async_computation.1 | async-start | bytes 131072 | tf_op jit(solution)/shard_map/all_to_all | solution.py:17
  34.6 0.0 reduce-scatter.2.cloned.1.call-start
  34.7 0.8 dynamic_slice.6
  35.5 5.0 %all-to-all-done.1 = f32[16,1,1024]{2,1,0:T(1,128)S(1)} async-done(((f32[16,1,1024]{2,1,0:T(1,128)}), f32[16,1,1024]{2,1,0:T(1,128)S(1)}, u32[]{:S(2)}, u32[]{:S(2)}) %all-to-all-start.1) | async-done | bytes 65568 | tf_op jit(solution)/shard_map/all_to_all | solution.py:17
  40.5 0.1 reduce_sum.64
  40.5 0.2 fusion.22
  40.7 0.2 copy.40
  41.0 1.1 stack.2
  42.1 97.1 %all_to_all.28 = bf16[16,1024,256]{1,2,0:T(8,128)(2,1)S(1)} all-to-all(bf16[16,1024,256]{1,2,0:T(8,128)(2,1)S(1)} %stack.2), channel_id=1, replica_groups=mesh['segment'=8,'tp'=16] {'tp'}, dimensions={0} | all-to-all | bytes 16777216 | tf_op jit(solution)/shard_map/all_to_all | solution.py:56
  139.2 0.0 copy-done
  139.2 2.4 fusion.16
  141.6 1.1 copy-done.2
  142.7 0.0 copy-done.6
  142.7 2.4 fusion.13
  145.1 0.0 copy-done.8
  145.1 0.0 copy-start.11
  145.1 0.0 copy-start.13
  145.1 0.8 multiply_reduce_fusion
  145.9 0.0 copy-start.3
  145.9 0.7 fusion.5
  146.6 0.0 copy-done.13
  146.7 1.0 convolution_convert_fusion
  147.6 0.0 copy-done.11
  147.6 1.5 fusion
  149.1 0.0 copy-done.3
  149.1 1.3 fusion.3
  150.4 0.0 copy-start.5
  150.4 1.3 copy-done.5
  151.7 0.7 convolution_convert_fusion.1
  152.4 0.0 copy-start.9
  152.4 8.1 %fusion.6 = f32[1024,4096]{1,0:T(8,128)} fusion(bf16[1024,256]{1,0:T(8,128)(2,1)S(1)} %convolution_convert_fusion.1, bf16[1,4096,256]{2,1,0:T(8,128)(2,1)S(1)} %copy-done), kind=kOutput, calls=%fused_computation.14 | convolution fusion | flops 2147483648 | bytes 19398656 | tf_op jit(solution)/shard_map/sc,dc->sd/dot_general | solution.py:97
  160.5 0.0 copy-done.9
  160.5 11.4 %add_convert_fusion = bf16[1024,4096]{1,0:T(8,128)(2,1)} fusion(f32[1024,4096]{1,0:T(8,128)} %fusion.6, bf16[1024,256]{1,0:T(8,128)(2,1)S(1)} %convolution_convert_fusion, bf16[1,4096,256]{2,1,0:T(8,128)(2,1)S(1)} %copy-done.6), kind=kOutput, calls=%fused_computation | convolution fusion | flops 2155872256 | bytes 27787264 | tf_op jit(solution)/shard_map/sc,dc->sd/dot_general | solution.py:101
  171.9 0.0 reduce-scatter.2.cloned.1.call-update
  172.0 0.1 dynamic_slice.7
  172.0 0.9 copy-done.10
  173.0 7.7 %convolution_bitcast_fusion.1 = f32[1,4096,256]{2,1,0:T(8,128)} fusion(bf16[1024,4096]{0,1:T(8,128)(2,1)} %bitcast.95, bf16[1024,256]{1,0:T(8,128)(2,1)S(1)} %copy-done.10), kind=kOutput, calls=%fused_computation.2 | convolution fusion | flops 2147483648 | bytes 13107200 | tf_op jit(solution)/shard_map/sd,sc->dc/dot_general | solution.py:95
  180.7 101.5 %reduce-scatter.2.cloned.1.call-done = bf16[128,4096]{1,0:T(8,128)(2,1)} async-done(((bf16[1024,4096]{1,0:T(8,128)(2,1)}), bf16[128,4096]{1,0:T(8,128)(2,1)}) %reduce-scatter.2.cloned.1.call-update) | async-done | bytes 1048592 | tf_op jit(solution)/shard_map/reduce_scatter | solution.py:98
  282.2 2.4 copy.49
  284.6 5.7 %all-to-all-start.3 = ((bf16[16,128,256]{2,1,0:T(8,128)(2,1)}), bf16[16,128,256]{2,1,0:T(8,128)(2,1)}, u32[]{:S(2)}, u32[]{:S(2)}) async-start(bf16[16,128,256]{2,1,0:T(8,128)(2,1)} %bitcast.92), calls=%async_computation.4 | async-start | bytes 2097152 | tf_op jit(solution)/shard_map/all_to_all | solution.py:35
  290.4 0.0 copy-start.12
  290.4 7.9 %convolution_bitcast_fusion = f32[1,4096,256]{2,1,0:T(8,128)} fusion(bf16[1024,4096]{0,1:T(8,128)(2,1)} %bitcast.96, bf16[1024,256]{1,0:T(8,128)(2,1)S(1)} %convolution_convert_fusion), kind=kOutput, calls=%fused_computation.1 | convolution fusion | flops 2147483648 | bytes 13107200 | tf_op jit(solution)/shard_map/sd,sc->dc/dot_general | solution.py:96
  298.3 0.0 copy-done.4
  298.3 0.0 copy-done.12
  298.3 1.9 fusion.19
  300.2 6.1 %all-to-all-done.3 = bf16[16,128,256]{2,1,0:T(8,128)(2,1)} async-done(((bf16[16,128,256]{2,1,0:T(8,128)(2,1)}), bf16[16,128,256]{2,1,0:T(8,128)(2,1)}, u32[]{:S(2)}, u32[]{:S(2)}) %all-to-all-start.3) | async-done | bytes 1048608 | tf_op jit(solution)/shard_map/all_to_all | solution.py:35
  306.3 1.4 convert_reduce_fusion
  307.7 0.0 copy-done.7
  307.7 0.2 multiply_reduce_fusion.2
  307.9 0.6 broadcast_in_dim.31
  308.5 4.1 %all-to-all-start.4 = ((f32[16,1,128]{2,1,0:T(1,128)}), f32[16,1,128]{2,1,0:T(1,128)S(1)}, u32[]{:S(2)}, u32[]{:S(2)}) async-start(f32[16,1,128]{2,1,0:T(1,128)} %broadcast_in_dim.31), calls=%async_computation.5 | async-start | bytes 16384 | tf_op jit(solution)/shard_map/all_to_all | solution.py:17
  312.6 2.3 fusion.20
  314.9 2.0 copy.44
  317.0 1.0 copy.45
  318.0 0.1 all-to-all-done.4
  318.1 0.8 subtract_multiply_fusion
  318.9 0.0 copy-done.1
  (10 shorter events, 0.0 us)
Async XLA Ops:
  7.2 132.0 %copy-start = (bf16[1,4096,256]{2,1,0:T(8,128)(2,1)S(1)}, bf16[1,4096,256]{2,1,0:T(8,128)(2,1)}, u32[]{:S(2)}) copy-start(bf16[1,4096,256]{2,1,0:T(8,128)(2,1)} %param.9) | copy-start | bytes 6291460
  27.4 13.0 %all-to-all-start.1 = ((f32[16,1,1024]{2,1,0:T(1,128)}), f32[16,1,1024]{2,1,0:T(1,128)S(1)}, u32[]{:S(2)}, u32[]{:S(2)}) async-start(f32[16,1,1024]{2,1,0:T(1,128)} %broadcast_in_dim.28), calls=%async_computation.1 | async-start | bytes 131072 | tf_op jit(solution)/shard_map/all_to_all | solution.py:17
  34.6 247.6 %reduce-scatter.2.cloned.1.call-start = ((), (), s32[]{:S(2)}) async-start(), calls=%async_computation.6 | async-start | bytes 9437184 | tf_op jit(solution)/shard_map/reduce_scatter | solution.py:98
  139.2 3.5 %copy-start.2 = (bf16[16,1024,256]{1,2,0:T(8,128)(2,1)}, bf16[16,1024,256]{1,2,0:T(8,128)(2,1)S(1)}, u32[]{:S(2)}) copy-start(bf16[16,1024,256]{1,2,0:T(8,128)(2,1)S(1)} %all_to_all.28) | copy-start | bytes 25165828
  139.2 3.5 %copy-start.6 = (bf16[1,4096,256]{2,1,0:T(8,128)(2,1)S(1)}, bf16[1,4096,256]{2,1,0:T(8,128)(2,1)}, u32[]{:S(2)}) copy-start(bf16[1,4096,256]{2,1,0:T(8,128)(2,1)} %param.10) | copy-start | bytes 6291460
  142.7 2.4 copy-start.8
  145.1 2.5 copy-start.11
  145.1 1.5 copy-start.13
  145.9 3.2 copy-start.3
  150.4 1.3 copy-start.5
  152.4 8.1 %copy-start.9 = (bf16[1024,256]{1,0:T(8,128)(2,1)}, bf16[1024,256]{1,0:T(8,128)(2,1)S(1)}, u32[]{:S(2)}) copy-start(bf16[1024,256]{1,0:T(8,128)(2,1)S(1)} %convolution_convert_fusion.1) | copy-start | bytes 1572868
  171.9 1.0 copy-start.10
  284.6 21.7 %all-to-all-start.3 = ((bf16[16,128,256]{2,1,0:T(8,128)(2,1)}), bf16[16,128,256]{2,1,0:T(8,128)(2,1)}, u32[]{:S(2)}, u32[]{:S(2)}) async-start(bf16[16,128,256]{2,1,0:T(8,128)(2,1)} %bitcast.92), calls=%async_computation.4 | async-start | bytes 2097152 | tf_op jit(solution)/shard_map/all_to_all | solution.py:35
  290.4 7.9 %copy-start.4 = (f32[1024,1024]{1,0:T(8,128)S(1)}, f32[1024,1024]{1,0:T(8,128)}, u32[]{:S(2)}) copy-start(f32[1024,1024]{1,0:T(8,128)} %copy-done.3) | copy-start | bytes 12582916
  290.4 7.9 %copy-start.12 = (bf16[1024,256]{1,0:T(8,128)(2,1)S(1)}, bf16[1024,256]{1,0:T(8,128)(2,1)}, u32[]{:S(2)}) copy-start(bf16[1024,256]{1,0:T(8,128)(2,1)} %copy-done.11) | copy-start | bytes 1572868
  298.3 9.4 %copy-start.7 = (bf16[128,256]{1,0:T(8,128)(2,1)S(1)}, bf16[128,256]{1,0:T(8,128)(2,1)}, u32[]{:S(2)}) copy-start(bf16[128,256]{1,0:T(8,128)(2,1)} %param.6) | copy-start | bytes 196612
  298.3 20.6 %copy-start.1 = (bf16[1,4096,256]{2,1,0:T(8,128)(2,1)S(1)}, bf16[1,4096,256]{2,1,0:T(8,128)(2,1)}, u32[]{:S(2)}) copy-start(bf16[1,4096,256]{2,1,0:T(8,128)(2,1)} %param.9) | copy-start | bytes 6291460
  308.5 9.6 %all-to-all-start.4 = ((f32[16,1,128]{2,1,0:T(1,128)}), f32[16,1,128]{2,1,0:T(1,128)S(1)}, u32[]{:S(2)}, u32[]{:S(2)}) async-start(f32[16,1,128]{2,1,0:T(1,128)} %broadcast_in_dim.31), calls=%async_computation.5 | async-start | bytes 16384 | tf_op jit(solution)/shard_map/all_to_all | solution.py:17
Sparse Core Ops, SparseCore 0:
  172.1 110.1 reduce-scatter.1
